TPU v7x, 128 devices: a whole 4x4x4 slice. The times are simulated.
128 devices in a mesh: ctx: 32 (over y, z, x_lo), ch: 4 (over x_hi, core).
Axes of the slice: x: 4 (x_hi: 2, x_lo: 2; x = x_hi * 2 + x_lo), y: 4, z: 4, core: 2. Of those that a mesh axis runs over, the one named last changes fastest.
Arguments:
- signal: bfloat16 [256, 512, 1024], P('ctx', None, 'ch'), may hold values from -15 to 15
- factor_first: bfloat16 [4, 512, 512], P('ch'), may hold values from -0.25 to 0.25
- factor_second: bfloat16 [4, 256, 256], P('ch'), may hold values from -0.375 to 0.375
- up_weight: bfloat16 [4, 256, 1024], P('ch'), may hold values from -0.375 to 0.375
- down_weight: bfloat16 [4, 1024, 256], P('ch'), may hold values from -0.1875 to 0.1875
- norm_gain: float32 [4, 256], P('ch'), may hold values from 0.1 to 1.9
- cotangent: bfloat16 [512, 256, 1024], P('ctx', None, 'ch'), may hold values from -6 to 6
Outputs:
- layer_out: bfloat16 [512, 256, 1024], P('ctx', None, 'ch')
- grad_signal: bfloat16 [256, 512, 1024], P('ctx', None, 'ch')
- grad_first: float32 [4, 512, 512], P('ch', 'ctx')
- grad_second: float32 [4, 256, 256], P('ch', 'ctx')
- grad_up: float32 [4, 256, 1024], P('ch', 'ctx')
- grad_down: float32 [4, 1024, 256], P('ch', 'ctx')
- grad_gain: float32 [4, 256], P('ch', 'ctx')
All inputs are finite; a program needn't handle non-finite values.
Results may differ from a plain program's by a relative error of at most 0.0095.
Values may be sent and summed in bfloat16 or wider, within the bound.
A program may use at most 128 MiB of HBM per device.

v0:
```python
import jax
import jax.numpy as jnp
from jax import lax
from jax.sharding import PartitionSpec as P

D = 1024
NB = 512
NA = 256


EPSILON = 1e-05


def transpose_slab(block):
    return lax.all_to_all(block, "ctx", split_axis=1, concat_axis=0, tiled=True)


def channel_total(partial_value):
    return lax.psum(partial_value, "ch")


def shards(signal, factor_first, factor_second, up_weight, down_weight, norm_gain, cotangent):
    groups = factor_first.shape[0]
    group_width = up_weight.shape[1]
    local_rows = signal.shape[0]
    row_count = signal.shape[1]
    inputs = signal.reshape(local_rows, row_count, groups, group_width)
    first_mix = jnp.einsum(
        "abgc,gbj->ajgc", inputs, factor_first, preferred_element_type=jnp.float32
    )
    gate_open = jax.nn.sigmoid(inputs.astype(jnp.float32))
    gated_rows = (first_mix * gate_open).astype(jnp.bfloat16)
    moved_rows = transpose_slab(gated_rows)
    mixed_rows = jnp.einsum(
        "ajgc,gai->jigc", moved_rows, factor_second, preferred_element_type=jnp.float32
    )
    mean_square = channel_total(jnp.sum(mixed_rows * mixed_rows, axis=(2, 3))) / D
    inverse = lax.rsqrt(mean_square + EPSILON)[:, :, None, None]
    gain_rows = norm_gain[None, None]
    normed = (mixed_rows * inverse * gain_rows).astype(jnp.bfloat16)
    preact = jnp.einsum("jigc,gch->jigh", normed, up_weight, preferred_element_type=jnp.float32)
    activation, gelu_back = jax.vjp(jax.nn.gelu, preact)
    act_rows = activation.astype(jnp.bfloat16)
    layer_out = (
        mixed_rows
        + jnp.einsum("jigh,ghc->jigc", act_rows, down_weight, preferred_element_type=jnp.float32)
    ).astype(jnp.bfloat16)
    upstream = cotangent.reshape(mixed_rows.shape)
    grad_act = jnp.einsum(
        "jigc,ghc->jigh", upstream, down_weight, preferred_element_type=jnp.float32
    )
    grad_pre = gelu_back(grad_act)[0].astype(jnp.bfloat16)
    grad_down = jnp.einsum("jigh,jigc->ghc", act_rows, upstream, preferred_element_type=jnp.float32)
    grad_up = jnp.einsum("jigc,jigh->gch", normed, grad_pre, preferred_element_type=jnp.float32)
    grad_normed = jnp.einsum(
        "jigh,gch->jigc", grad_pre, up_weight, preferred_element_type=jnp.float32
    )
    grad_gain = jnp.sum(grad_normed * mixed_rows * inverse, axis=(0, 1))
    grad_scaled = grad_normed * gain_rows
    cross = channel_total(jnp.sum(grad_scaled * mixed_rows, axis=(2, 3))) / D
    grad_mixed = (
        upstream.astype(jnp.float32)
        + inverse * grad_scaled
        - inverse**3 * mixed_rows * cross[:, :, None, None]
    ).astype(jnp.bfloat16)
    grad_second = jnp.einsum(
        "ajgc,jigc->gai", moved_rows, grad_mixed, preferred_element_type=jnp.float32
    )
    grad_moved = jnp.einsum(
        "jigc,gai->jagc", grad_mixed, factor_second, preferred_element_type=jnp.float32
    ).astype(jnp.bfloat16)
    grad_gated = jnp.swapaxes(transpose_slab(grad_moved), 0, 1)
    gated_float = grad_gated.astype(jnp.float32)
    grad_first_mix = (gated_float * gate_open).astype(jnp.bfloat16)
    grad_gate = gated_float * first_mix * gate_open * (1.0 - gate_open)
    grad_input = (
        jnp.einsum(
            "ajgc,gbj->abgc", grad_first_mix, factor_first, preferred_element_type=jnp.float32
        )
        + grad_gate
    ).astype(jnp.bfloat16)
    grad_first = jnp.einsum(
        "abgc,ajgc->gbj", inputs, grad_first_mix, preferred_element_type=jnp.float32
    )
    summed = (
        lax.psum_scatter(grad_first, "ctx", scatter_dimension=1, tiled=True),
        lax.psum_scatter(grad_second, "ctx", scatter_dimension=1, tiled=True),
        lax.psum_scatter(grad_up, "ctx", scatter_dimension=1, tiled=True),
        lax.psum_scatter(grad_down, "ctx", scatter_dimension=1, tiled=True),
        lax.psum_scatter(grad_gain, "ctx", scatter_dimension=1, tiled=True),
    )
    grad_scale = (NA * NB) ** (-0.5)
    return (
        layer_out.reshape(cotangent.shape),
        grad_input.reshape(signal.shape),
        summed[0] * grad_scale,
        summed[1] * grad_scale,
        summed[2] * grad_scale,
        summed[3] * grad_scale,
        summed[4] * grad_scale,
    )


def solution(mesh):
    placed = (
        P("ctx", None, "ch"),
        P("ch", None, None),
        P("ch", None, None),
        P("ch", None, None),
        P("ch", None, None),
        P("ch", None),
        P("ctx", None, "ch"),
    )
    return jax.shard_map(
        shards,
        mesh=mesh,
        in_specs=placed,
        out_specs=(
            P("ctx", None, "ch"),
            P("ctx", None, "ch"),
            P("ch", "ctx", None),
            P("ch", "ctx", None),
            P("ch", "ctx", None),
            P("ch", "ctx", None),
            P("ch", "ctx"),
        ),
        check_vma=False,
    )
```

profile of v0, /device:TPU:0, one launch (start us, length us, event | category | flops | bytes accessed | tf_op | source)
XLA Modules:
  0.0 933.3 jit_solution(12481058364752827710)
XLA Ops:
  7.2 6.1 fusion.25
  13.3 2.5 copy.66
  15.8 9.4 %all-to-all-start = ((bf16[8,512,1,256]{3,0,2,1:T(8,128)(2,1)}), bf16[8,512,1,256]{3,0,2,1:T(8,128)(2,1)S(1)}, u32[]{:S(2)}, u32[]{:S(2)}) async-start(bf16[8,512,1,256]{3,0,2,1:T(8,128)(2,1)} %copy.66), calls=%async_computation | async-start | bytes 4194304 | tf_op jit(solution)/shard_map/all_to_all | solution.py:15
  25.2 0.0 reduce-scatter.5.cloned.1.call-start
  25.3 3.9 copy.72
  29.2 28.2 %all-to-all-done = bf16[8,512,1,256]{3,0,2,1:T(8,128)(2,1)S(1)} async-done(((bf16[8,512,1,256]{3,0,2,1:T(8,128)(2,1)}), bf16[8,512,1,256]{3,0,2,1:T(8,128)(2,1)S(1)}, u32[]{:S(2)}, u32[]{:S(2)}) %all-to-all-start) | async-done | bytes 2097184 | tf_op jit(solution)/shard_map/all_to_all | solution.py:15
  57.4 0.4 copy.67
  57.8 0.3 copy.68
  58.1 1.3 copy-done.5
  59.4 4.0 fusion.28
  63.4 13.3 %psum.14 = f32[16,256]{1,0:T(8,128)S(1)} all-reduce(f32[16,256]{1,0:T(8,128)S(1)} %get-tuple-element.41), channel_id=1, replica_groups=mesh['ctx'=32,'ch'=4] {'ch'}, use_global_device_ids=true, to_apply=%region_1.0 | all-reduce | flops 4096 | bytes 32768 | tf_op jit(solution)/shard_map/psum | solution.py:19
  76.7 0.6 multiply_multiply_fusion.2
  77.4 4.8 fusion.68
  82.2 15.0 %fusion.6 = bf16[16,256,1,1024]{3,1,0,2:T(8,128)(2,1)} fusion(f32[16,256,1024]{2,1,0:T(8,128)S(1)} %fusion.68, bf16[16,256,256]{2,1,0:T(8,128)(2,1)S(1)} %copy-done.4, bf16[1,1024,256]{2,1,0:T(8,128)(2,1)} %param.11), kind=kOutput, calls=%fused_computation.8 | convolution fusion | flops 2231369728 | bytes 27787264 | tf_op jit(solution)/shard_map/jigc,ghc->jigh/dot_general | solution.py:49
  97.2 9.5 %fusion.24 = (f32[256]{0:T(256)S(1)}, f32[16,256]{1,0:T(8,128)S(1)}, f32[16,256,256]{1,2,0:T(8,128)}) fusion(f32[16,256,256]{2,1,0:T(8,128)} %get-tuple-element.42, f32[16,256]{1,0:T(8,128)S(1)} %get-tuple-element.38, f32[256]{0:T(256)S(1)} %bitcast.261, bf16[1,256,1024]{2,1,0:T(8,128)(2,1)S(1)} %copy-done, bf16[16,256,1,1024]{3,1,0,2:T(8,128)(2,1)} %fusion.6), kind=kOutput, calls=%fused_computation.35 | convolution fusion | flops 2153770752 | bytes 17336320 | tf_op jit(solution)/shard_map/jigh,gch->jigc/dot_general | solution.py:55
  106.7 13.1 %psum.15 = f32[16,256]{1,0:T(8,128)S(1)} all-reduce(f32[16,256]{1,0:T(8,128)S(1)} %get-tuple-element.36), channel_id=1, replica_groups=mesh['ctx'=32,'ch'=4] {'ch'}, use_global_device_ids=true, to_apply=%region_3.0 | all-reduce | flops 4096 | bytes 32768 | tf_op jit(solution)/shard_map/psum | solution.py:19
  119.9 5.7 fusion.37
  125.6 2.0 fusion.59
  127.6 0.3 reduce-scatter.9.cloned.1.call-start
  127.9 10.3 %fusion.50 = f32[1,1024,256]{2,1,0:T(8,128)} fusion(bf16[16,256,256]{2,1,0:T(8,128)(2,1)} %param.13, f32[16,256,1024]{2,1,0:T(8,128)} %copy-done.2), kind=kOutput, calls=%fused_computation.65 | convolution fusion | flops 2185232384 | bytes 19922944 | tf_op jit(solution)/shard_map/jigh,jigc->ghc/dot_general | solution.py:53
  138.3 0.6 dynamic-slice
  140.1 2.1 convert_bitcast_fusion.1
  142.2 4.6 copy.75
  146.8 4.0 all-to-all-start.1
  150.8 0.0 reduce-scatter.7.cloned.1.call-start
  150.9 8.2 fusion.56
  159.1 0.0 all-reduce.4.cloned.1.call-start
  159.1 11.4 %fusion.36 = bf16[16,256,256]{1,2,0:T(8,128)(2,1)} fusion(f32[16,256,256]{2,1,0:T(8,128)} %get-tuple-element.42, f32[16,256,1024]{2,1,0:T(8,128)} %copy-done.2, bf16[1,1024,256]{2,1,0:T(8,128)(2,1)S(1)} %copy-done.13), kind=kOutput, calls=%fused_computation.54 | convolution fusion | flops 2187329536 | bytes 23592960 | tf_op jit(solution)/shard_map/jigh,ghc->jigc/dot_general | solution.py:46
  170.5 3.9 copy.84
  174.4 83.5 %all-reduce.1 = f32[1,256]{1,0:T(1,128)S(1)} all-reduce(f32[1,256]{1,0:T(1,128)S(1)} %bitcast.264), channel_id=6, replica_groups=mesh['ctx'=32,'ch'=4] {'ctx'}, use_global_device_ids=true, to_apply=%region_9.0.clone | all-reduce | flops 256 | bytes 2048
  257.9 0.6 fusion.72
  258.5 31.5 %reduce-scatter.5.cloned.1.call-done = f32[1,8,256]{2,1,0:T(8,128)} async-done(((f32[1,256,256]{2,1,0:T(8,128)}), f32[1,8,256]{2,1,0:T(8,128)}) %reduce-scatter.5.cloned.1.call-update) | async-done | bytes 8208 | tf_op jit(solution)/shard_map/reduce_scatter | solution.py:87
  290.0 1.3 broadcast_multiply_fusion.3
  291.3 0.7 convert_bitcast_fusion
  292.0 2.4 copy.77
  294.5 1.4 fusion.27
  295.9 0.5 copy-done.3
  296.4 1.3 copy-done.8
  297.7 2.3 fusion.53
  300.0 3.6 copy.80
  303.6 7.2 fusion.47
  310.8 143.2 %reduce-scatter.9.cloned.1.call-done = f32[1,32,256]{2,1,0:T(8,128)} async-done(((f32[1,1024,256]{2,1,0:T(8,128)}), f32[1,32,256]{2,1,0:T(8,128)}) %reduce-scatter.9.cloned.1.call-update) | async-done | bytes 32784 | tf_op jit(solution)/shard_map/reduce_scatter | solution.py:89
  454.0 1.4 broadcast_multiply_fusion
  455.4 160.5 %reduce-scatter.7.cloned.1.call-done = f32[1,8,1024]{2,1,0:T(8,128)} async-done(((f32[1,256,1024]{2,1,0:T(8,128)}), f32[1,8,1024]{2,1,0:T(8,128)}) %reduce-scatter.7.cloned.1.call-update) | async-done | bytes 32784 | tf_op jit(solution)/shard_map/reduce_scatter | solution.py:88
  615.9 1.4 broadcast_multiply_fusion.1
  617.3 308.0 %all-reduce.4.cloned.1.call-done = f32[1,512,512]{2,0,1:T(1,128)} async-done(((f32[1,512,512]{2,0,1:T(1,128)}), f32[1,512,512]{2,0,1:T(1,128)}) %all-reduce.4.cloned.1.call-update) | async-done | bytes 1048592
  925.3 0.8 dynamic-slice_multiply_fusion
  926.1 0.6 copy.85
  (35 shorter events, 0.2 us)
Async XLA Ops:
  7.2 70.2 %copy-start = (bf16[1,256,1024]{2,1,0:T(8,128)(2,1)S(1)}, bf16[1,256,1024]{2,1,0:T(8,128)(2,1)}, u32[]{:S(2)}) copy-start(bf16[1,256,1024]{2,1,0:T(8,128)(2,1)} %param.10) | copy-start | bytes 1572868
  15.8 41.5 %all-to-all-start = ((bf16[8,512,1,256]{3,0,2,1:T(8,128)(2,1)}), bf16[8,512,1,256]{3,0,2,1:T(8,128)(2,1)S(1)}, u32[]{:S(2)}, u32[]{:S(2)}) async-start(bf16[8,512,1,256]{3,0,2,1:T(8,128)(2,1)} %copy.66), calls=%async_computation | async-start | bytes 4194304 | tf_op jit(solution)/shard_map/all_to_all | solution.py:15
  25.2 264.8 %reduce-scatter.5.cloned.1.call-start = ((), (), s32[]{:S(2)}) async-start(), calls=%async_computation.5 | async-start | bytes 270336 | tf_op jit(solution)/shard_map/reduce_scatter | solution.py:87
  29.2 30.2 %copy-start.9 = (bf16[1,256,256]{2,1,0:T(8,128)(2,1)S(1)}, bf16[1,256,256]{2,1,0:T(8,128)(2,1)}, u32[]{:S(2)}) copy-start(bf16[1,256,256]{2,1,0:T(8,128)(2,1)} %param.9) | copy-start | bytes 393220
  58.1 1.3 copy-start.5
  58.1 19.3 %copy-start.12 = (f32[1,256]{1,0:T(1,128)S(1)}, f32[1,256]{1,0:T(1,128)}, u32[]{:S(2)}) copy-start(f32[1,256]{1,0:T(1,128)} %param.12) | copy-start | bytes 3076
  77.4 4.8 copy-start.4
  82.2 15.0 %copy-start.2 = (f32[16,256,1024]{2,1,0:T(8,128)}, f32[16,256,1024]{2,1,0:T(8,128)S(1)}, u32[]{:S(2)}) copy-start(f32[16,256,1024]{2,1,0:T(8,128)S(1)} %fusion.68) | copy-start | bytes 50331652
  97.2 22.6 %copy-start.11 = (f32[16,256]{1,0:T(8,128)S(1)}, f32[16,256]{1,0:T(8,128)}, u32[]{:S(2)}) copy-start(f32[16,256]{1,0:T(8,128)} %get-tuple-element.37) | copy-start | bytes 49156
  119.9 5.7 copy-start.6
  127.6 10.7 %copy-start.15 = (u32[128]{0:T(128)S(1)}, u32[128]{0:T(128)}, u32[]{:S(2)}) copy-start(u32[128]{0:T(128)} %constant.36) | copy-start | bytes 1540
  127.6 12.5 %copy-start.10 = (bf16[1,256,256]{2,1,0:T(8,128)(2,1)S(1)}, bf16[1,256,256]{2,1,0:T(8,128)(2,1)}, u32[]{:S(2)}) copy-start(bf16[1,256,256]{2,1,0:T(8,128)(2,1)} %param.9) | copy-start | bytes 393220
  127.6 326.4 %reduce-scatter.9.cloned.1.call-start = ((), (), s32[]{:S(2)}) async-start(), calls=%async_computation.7 | async-start | bytes 1081344 | tf_op jit(solution)/shard_map/reduce_scatter | solution.py:89
  146.8 144.5 %all-to-all-start.1 = ((bf16[16,256,1,256]{3,0,2,1:T(8,128)(2,1)}), bf16[16,256,1,256]{3,0,2,1:T(8,128)(2,1)S(1)}, u32[]{:S(2)}, u32[]{:S(2)}) async-start(bf16[16,256,1,256]{3,0,2,1:T(8,128)(2,1)} %copy.75), calls=%async_computation.1 | async-start | bytes 4194304 | tf_op jit(solution)/shard_map/all_to_all | solution.py:15
  150.8 8.3 copy-start.13
  150.8 465.1 %reduce-scatter.7.cloned.1.call-start = ((), (), s32[]{:S(2)}) async-start(), calls=%async_computation.6 | async-start | bytes 1081344 | tf_op jit(solution)/shard_map/reduce_scatter | solution.py:88
  159.1 766.3 %all-reduce.4.cloned.1.call-start = ((), (), s32[]{:S(2)}) async-start(), calls=%async_computation.8 | async-start | bytes 2097152
  292.0 2.5 copy-start.7
  294.5 1.9 copy-start.3
  296.4 1.3 copy-start.8
  297.7 5.9 copy-start.14
  303.6 623.1 %copy-start.1 = (bf16[1,256,1024]{2,1,0:T(8,128)(2,1)S(1)}, bf16[1,256,1024]{2,1,0:T(8,128)(2,1)}, u32[]{:S(2)}) copy-start(bf16[1,256,1024]{2,1,0:T(8,128)(2,1)} %param.10) | copy-start | bytes 1572868
Sparse Core Ops, SparseCore 0:
  127.7 162.2 reduce-scatter.4
  292.4 161.5 reduce-scatter.8
  456.3 159.4 reduce-scatter.6
  618.2 307.0 all-reduce.3
where the time goes:
time: 934 us; the launch traced here: 933 us
  waiting for transfers between devices  672 us (72%)
  blocking collectives  110 us (12%)
  matrix products  82.9 us (9%)
  local copies, waits for them, and re-layouts  26.1 us (3%)
  between operations  15.3 us (2%)
  starting transfers between devices  13.8 us (1%)
  other arithmetic  13.8 us (1%)
    unnamed x5, waiting for transfers between devices  308 us
    reduce_scatter x1, waiting for transfers between devices, shards(): lax.psum_scatter(grad_up, 'ctx', scatter_dimension=1, tiled=True)  161 us
    reduce_scatter x1, waiting for transfers between devices, shards(): lax.psum_scatter(grad_down, 'ctx', scatter_dimension=1, tiled=True)  143 us
    unnamed x1, blocking collectives  83.5 us
    reduce_scatter x1, waiting for transfers between devices, shards(): lax.psum_scatter(grad_second, 'ctx', scatter_dimension=1, tiled=True)  31.5 us
    all_to_all x2, waiting for transfers between devices, transpose_slab(): return lax.all_to_all(block, 'ctx', split_axis=1, concat_axis=0, tiled=True)  28.2 us
    psum x2, blocking collectives, channel_total(): return lax.psum(partial_value, 'ch')  26.4 us
  transfers between devices with their start and end apart: 6, of which 5 were waited for; matrix products, arithmetic and copies ran while one was open for 7% of the time, Pallas kernels for 0%

commit v1 on v0

v1 whole, which is shorter than its diff:
```python
import functools
import math

import jax
import jax.numpy as jnp
from jax import lax
from jax.experimental import pallas as pl
from jax.experimental.pallas import tpu as pltpu
from jax.sharding import PartitionSpec as P

D = 1024
EPSILON = 1e-05
CHUNKS = 4
LANES = 128
ROWS = 8
HIDDEN = 256
MESH = pl.DeviceIdType.MESH
BF16 = jnp.bfloat16
F32 = jnp.float32
CUBIC = 0.044715
SLOPE = math.sqrt(2.0 / math.pi)


def dot(lhs, rhs):
    return jnp.dot(lhs, rhs, preferred_element_type=F32)


def dot_rows(lhs, rhs):
    return lax.dot_general(lhs, rhs, (((0,), (0,)), ((), ())), preferred_element_type=F32)


def dot_columns(lhs, rhs):
    return lax.dot_general(lhs, rhs, (((1,), (1,)), ((), ())), preferred_element_type=F32)


def lane_blocks(value):
    return [value[..., at : at + LANES] for at in range(0, value.shape[-1], LANES)]


def kernel(
    groups, signal, first, second, up, down, gain, cotangent,
    layer_out, grad_signal, out_first, out_second, out_up, out_down, out_gain,
    first_t, second_t, up_t, down_t, first_mix, stage, send_one, recv_one, moved, mixed_all,
    scaled_all, squares, crosses, inverse_rows, inverse_wide, cross_wide, send_two, recv_two,
    unpacked, acc_up, acc_down, acc_second, acc_first, acc_gain, pack_one, got_one, pack_two,
    got_two, one_send, one_recv, two_send, two_recv, square_send, square_recv, cross_send,
    cross_recv, grad_send, grad_recv,
):
    me = lax.axis_index("ctx")
    channel = lax.axis_index("ch")
    local_a, positions, width = signal.shape
    local_j, rows, _ = cotangent.shape
    hidden = up.shape[1]
    size = rows // local_a
    span = local_j // CHUNKS
    block = stage.shape[1] // local_a - ROWS
    per_block = block // local_j
    blocks = positions // block
    pitch = block + ROWS
    chunk_rows = span * local_a
    halves = width // LANES
    grad_scale = 1.0 / math.sqrt(rows * positions)

    barrier = pltpu.get_barrier_semaphore()

    def greet(k, carry):
        pl.semaphore_signal(
            barrier, inc=1, device_id={"ctx": lax.rem(me + k, size)}, device_id_type=MESH
        )
        return carry

    lax.fori_loop(1, size, greet, 0)
    for k in range(1, groups):
        pl.semaphore_signal(
            barrier, inc=1, device_id={"ch": lax.rem(channel + k, groups)}, device_id_type=MESH
        )

    first_t[...] = first[...].T

    def send_first(target, q):
        part = pl.ds(pl.multiple_of(q * chunk_rows, chunk_rows), chunk_rows)

        @pl.when(target != me)
        def _():
            pltpu.make_async_remote_copy(
                src_ref=send_one.at[target, part],
                dst_ref=recv_one.at[me, part],
                send_sem=one_send,
                recv_sem=one_recv.at[q],
                device_id={"ctx": target},
                device_id_type=MESH,
            ).start()

        @pl.when(target == me)
        def _():
            pltpu.make_async_copy(
                send_one.at[me, part], recv_one.at[me, part], one_recv.at[q]
            ).start()

    def first_block(step, carry):
        at = lax.rem(me // per_block + step, blocks)
        part = pl.ds(pl.multiple_of(at * block, block), block)
        weights = first_t[part, :]
        for a in range(local_a):
            mix = dot(weights, signal[a])
            first_mix[a, part, :] = mix
            gated = mix * lax.logistic(signal[a, part, :].astype(F32))
            for h, piece in enumerate(lane_blocks(gated)):
                stage[h, a * pitch : a * pitch + block, :] = piece

        def turn(k, inner):
            for h in range(halves):
                taken = [
                    stage.at[h][pl.ds(k * local_j + j, local_a, stride=pitch), :]
                    for j in range(local_j)
                ]
                send_one[at * per_block + k, :, h * LANES : (h + 1) * LANES] = jnp.concatenate(
                    taken, axis=0
                ).astype(BF16)
            return inner

        lax.fori_loop(0, per_block, turn, 0)

        @pl.when(step == 0)
        def _():
            pl.semaphore_wait(barrier, size - 1 + groups - 1)

        def launch(k, inner):
            send_first(at * per_block + lax.rem(me + k, per_block), 0)
            return inner

        lax.fori_loop(0, per_block, launch, 0)
        return carry

    lax.fori_loop(0, blocks, first_block, 0)

    def launch_rest(k, carry):
        send_first(lax.rem(me + lax.rem(k, size), size), 1 + k // size)
        return carry

    lax.fori_loop(0, size * (CHUNKS - 1), launch_rest, 0)

    second_t[...] = second[...].T
    up_t[...] = up[...].T
    down_t[...] = down[...].T
    acc_up[...] = jnp.zeros_like(acc_up)
    acc_down[...] = jnp.zeros_like(acc_down)
    acc_second[...] = jnp.zeros_like(acc_second)
    acc_gain[...] = jnp.zeros_like(acc_gain)

    lane = lax.broadcasted_iota(jnp.int32, (rows, LANES), 1)

    def exchange(table, q, columns, send_sem, recv_sem):
        table[q, channel] = columns.T[:ROWS]
        for k in range(1, groups):
            pltpu.make_async_remote_copy(
                src_ref=table.at[q, channel],
                dst_ref=table.at[q, channel],
                send_sem=send_sem,
                recv_sem=recv_sem.at[q],
                device_id={"ch": lax.rem(channel + k, groups)},
                device_id_type=MESH,
            ).start()

    def collect(table, q, recv_sem):
        if groups > 1:
            others = table.at[q, : groups - 1]
            pltpu.make_async_copy(others, others, recv_sem.at[q]).wait()
        total = table[q, 0]
        for k in range(1, groups):
            total = total + table[q, k]
        return total / D

    def spread(values, wide):
        tall = jnp.concatenate([values] * (LANES // ROWS), axis=0).T
        for k in range(span):
            wide[k] = jnp.broadcast_to(tall[:, k : k + 1], (rows, LANES))

    def mix_chunk(q):
        part = pl.ds(pl.multiple_of(q * chunk_rows, chunk_rows), chunk_rows)
        arrived = recv_one.at[:, part]
        pltpu.make_async_copy(arrived, arrived, one_recv.at[q]).wait()
        columns = jnp.zeros((rows, LANES), F32)
        for pair in range(span // 2):
            at = pl.multiple_of(q * chunk_rows + pair * 2 * local_a, 2 * local_a)
            both = recv_one[:, pl.ds(at, 2 * local_a), :].astype(F32)
            for odd in range(2):
                k = 2 * pair + odd
                rows_k = both[:, odd * local_a : (odd + 1) * local_a, :]
                rows_k = rows_k.reshape(rows, width).astype(BF16)
                moved[q * span + k] = rows_k
                mixed = dot(second_t[...], rows_k)
                mixed_all[q * span + k] = mixed
                total = jnp.sum(mixed * mixed, axis=1, keepdims=True)
                columns = jnp.where(lane == k, total, columns)
        exchange(squares, q, columns, square_send, square_recv)

    def mlp_chunk(q):
        inverse = lax.rsqrt(collect(squares, q, square_recv) + EPSILON)
        inverse_rows[...] = inverse
        spread(inverse, inverse_wide)

        def tile(k, columns):
            j = q * span + k
            mixed = mixed_all[j]
            wide = jnp.concatenate([inverse_wide[k]] * halves, axis=1)
            scaled = mixed * wide
            gains = gain[...]
            normed = (scaled * gains).astype(BF16)
            upstream = cotangent[j]
            out = mixed
            grad_normed = jnp.zeros((rows, width), F32)
            for at in range(0, hidden, HIDDEN):
                part = slice(at, at + HIDDEN)
                pre = dot(normed, up[:, part])
                grad_act = dot(upstream, down_t[:, part])
                square = pre * pre
                curve = jnp.tanh(pre * (SLOPE + (SLOPE * CUBIC) * square))
                half = 0.5 + 0.5 * curve
                act = (pre * half).astype(BF16)
                bend = (1.0 - curve * curve) * pre
                slope = half + bend * (0.5 * SLOPE + (1.5 * SLOPE * CUBIC) * square)
                grad_pre = (grad_act * slope).astype(BF16)
                out = out + dot(act, down[part, :])
                grad_normed = grad_normed + dot(grad_pre, up_t[part, :])
                acc_down[:, part] += dot_rows(upstream, act)
                acc_up[:, part] += dot_rows(normed, grad_pre)
            layer_out[j] = out.astype(BF16)
            acc_gain[...] += jnp.sum(
                (grad_normed * scaled).reshape(rows // ROWS, ROWS, width), axis=0
            )
            grad_scaled = grad_normed * gains
            scaled_all[j] = grad_scaled
            total = jnp.sum(grad_scaled * mixed, axis=1, keepdims=True)
            return jnp.where(lane == k, total, columns)

        columns = lax.fori_loop(0, span, tile, jnp.zeros((rows, LANES), F32))
        exchange(crosses, q, columns, cross_send, cross_recv)

    def back_chunk(q):
        inverse = inverse_rows[...]
        spread(collect(crosses, q, cross_recv) * inverse * inverse * inverse, cross_wide)
        for pair in range(span // 2):
            turned = []
            for odd in range(2):
                k = 2 * pair + odd
                j = q * span + k
                wide = jnp.concatenate([inverse_wide[k]] * halves, axis=1)
                pull = jnp.concatenate([cross_wide[k]] * halves, axis=1)
                grad_mixed = (
                    cotangent[j].astype(F32) + wide * scaled_all[j] - pull * mixed_all[j]
                ).astype(BF16)
                acc_second[...] += dot_columns(moved[j], grad_mixed)
                turned.append(dot(second[...], grad_mixed).reshape(size, local_a, width))
            send_two[:, q * (span // 2) + pair] = jnp.concatenate(turned, axis=1).astype(BF16)

        pairs = pl.ds(q * (span // 2), span // 2)

        def launch(k, carry):
            target = lax.rem(me + k, size)
            pltpu.make_async_remote_copy(
                src_ref=send_two.at[target, pairs],
                dst_ref=recv_two.at[me, pairs],
                send_sem=two_send,
                recv_sem=two_recv.at[q],
                device_id={"ctx": target},
                device_id_type=MESH,
            ).start()
            return carry

        lax.fori_loop(1, size, launch, 0)
        pltpu.make_async_copy(
            send_two.at[me, pairs], recv_two.at[me, pairs], two_recv.at[q]
        ).start()

    mix_chunk(0)

    def chunk(q, carry):
        mlp_chunk(q)

        @pl.when(q < CHUNKS - 1)
        def _():
            mix_chunk(q + 1)

        back_chunk(q)
        return carry

    lax.fori_loop(0, CHUNKS, chunk, 0)

    def scatter(pack, got, index):
        def launch(k, carry):
            target = lax.rem(me + k, size)
            pltpu.make_async_remote_copy(
                src_ref=pack.at[target],
                dst_ref=got.at[me],
                send_sem=grad_send.at[index],
                recv_sem=grad_recv.at[index],
                device_id={"ctx": target},
                device_id_type=MESH,
            ).start()
            return carry

        lax.fori_loop(1, size, launch, 0)
        pltpu.make_async_copy(pack.at[me], got.at[me], grad_recv.at[index]).start()

    def gather(got, index):
        pltpu.make_async_copy(got, got, grad_recv.at[index]).wait()

        def add(k, total):
            return total + got[k].astype(F32)

        return lax.fori_loop(0, size, add, jnp.zeros(got.shape[1:], F32)) * grad_scale

    ups = lane_blocks(acc_up[...].reshape(size, width // size, hidden))
    seconds = lane_blocks(acc_second[...].reshape(size, local_a, rows))
    downs = lane_blocks(acc_down[...].T.reshape(size, hidden // size, width))
    gain_row = jnp.sum(acc_gain[...], axis=0, keepdims=True)
    gains = [
        jnp.broadcast_to(piece[None], (size, ROWS, LANES)) for piece in lane_blocks(gain_row)
    ]
    pieces = ups + seconds + downs + gains
    pieces = pieces + [gains[0]] * (len(pieces) % 2)
    at = 0
    while pieces:
        joined = pieces.pop(0)
        if joined.shape[1] % 16:
            joined = jnp.concatenate([joined, pieces.pop(0)], axis=1)
        pack_one[:, at : at + joined.shape[1], :] = joined.astype(BF16)
        at += joined.shape[1]
    scatter(pack_one, got_one, 0)

    pltpu.make_async_copy(recv_two, recv_two, two_recv.at[0]).wait() if CHUNKS == 1 else None
    if CHUNKS > 1:
        for q in range(CHUNKS):
            arrived = recv_two.at[:, q * (span // 2) : (q + 1) * (span // 2)]
            pltpu.make_async_copy(arrived, arrived, two_recv.at[q]).wait()

    def unpack(k, carry):
        value = recv_two[k].astype(F32).reshape(local_j * local_a, width)
        part = pl.ds(pl.multiple_of(k * local_j * local_a, local_j * local_a), local_j * local_a)
        for h, piece in enumerate(lane_blocks(value)):
            unpacked[h, part, :] = piece
        return carry

    lax.fori_loop(0, size, unpack, 0)
    acc_first[...] = jnp.zeros_like(acc_first)

    def back_row(a, carry):
        grad_gated = jnp.concatenate(
            [unpacked.at[h][pl.ds(a, positions, stride=local_a), :] for h in range(halves)], axis=1
        )
        inputs = signal[a]
        gate = lax.logistic(inputs.astype(F32))
        opened = grad_gated * gate
        grad_mix = opened.astype(BF16)
        grad_gate = opened * first_mix[a] * (1.0 - gate)
        grad_signal[a] = (dot(first[...], grad_mix) + grad_gate).astype(BF16)
        acc_first[...] += dot_columns(inputs, grad_mix)
        return carry

    lax.fori_loop(0, local_a, back_row, 0)
    pack_two[...] = acc_first[...].reshape(pack_two.shape).astype(BF16)
    scatter(pack_two, got_two, 1)

    total = gather(got_one, 0)
    at = 0
    for out in (out_up, out_second, out_down):
        height = out.shape[0]
        for h in range(out.shape[1] // LANES):
            out[:, h * LANES : (h + 1) * LANES] = total[at : at + height]
            at += height
    gain_sum = jnp.concatenate(
        [total[at + h * ROWS : at + (h + 1) * ROWS] for h in range(halves)], axis=1
    )
    turn = lax.rem(width - me * (width // size), width)
    out_gain[...] = pltpu.roll(gain_sum, turn, 1)[:, :LANES]
    out_first[...] = gather(got_two, 1)

    def drain(ref, sem):
        pltpu.make_async_copy(ref, ref, sem).wait()

    drain(send_one.at[: size - 1], one_send)
    drain(send_two.at[: size - 1], two_send)
    drain(pack_one.at[: size - 1], grad_send.at[0])
    drain(pack_two.at[: size - 1], grad_send.at[1])
    if groups > 1:
        drain(squares.at[:, : groups - 1], square_send)
        drain(crosses.at[:, : groups - 1], cross_send)


def shards(mesh, signal, factor_first, factor_second, up_weight, down_weight, norm_gain, cotangent):
    size, groups = mesh.shape["ctx"], mesh.shape["ch"]
    local_a, positions, width = signal.shape
    local_j, rows, _ = cotangent.shape
    hidden = up_weight.shape[2]
    halves = width // LANES
    span = local_j // CHUNKS
    block = min(128, positions)
    vmem = pl.BlockSpec(memory_space=pltpu.VMEM)
    packed = (
        width // size * (hidden // LANES)
        + local_a * (rows // LANES)
        + hidden // size * halves
        + ROWS * halves
    )
    packed += packed % 16

    def out(shape, dtype):
        return jax.ShapeDtypeStruct(shape, dtype)

    outs = (
        out(cotangent.shape, BF16),
        out(signal.shape, BF16),
        out((positions // size, positions), F32),
        out((rows // size, rows), F32),
        out((width // size, hidden), F32),
        out((hidden // size, width), F32),
        out((ROWS, LANES), F32),
    )
    dma = pltpu.SemaphoreType.DMA
    scratch = [
        pltpu.VMEM((positions, positions), BF16),
        pltpu.VMEM((rows, rows), BF16),
        pltpu.VMEM((hidden, width), BF16),
        pltpu.VMEM((width, hidden), BF16),
        pltpu.VMEM((local_a, positions, width), F32),
        pltpu.VMEM((halves, local_a * (block + ROWS), LANES), F32),
        pltpu.VMEM((size, local_j * local_a, width), BF16),
        pltpu.VMEM((size, local_j * local_a, width), BF16),
        pltpu.VMEM((local_j, rows, width), BF16),
        pltpu.VMEM((local_j, rows, width), F32),
        pltpu.VMEM((local_j, rows, width), F32),
        pltpu.VMEM((CHUNKS, groups, ROWS, rows), F32),
        pltpu.VMEM((CHUNKS, groups, ROWS, rows), F32),
        pltpu.VMEM((ROWS, rows), F32),
        pltpu.VMEM((span, rows, LANES), F32),
        pltpu.VMEM((span, rows, LANES), F32),
        pltpu.VMEM((size, local_j // 2, 2 * local_a, width), BF16),
        pltpu.VMEM((size, local_j // 2, 2 * local_a, width), BF16),
        pltpu.VMEM((halves, positions * local_a, LANES), F32),
        pltpu.VMEM((width, hidden), F32),
        pltpu.VMEM((width, hidden), F32),
        pltpu.VMEM((rows, rows), F32),
        pltpu.VMEM((positions, positions), F32),
        pltpu.VMEM((ROWS, width), F32),
        pltpu.VMEM((size, packed, LANES), BF16),
        pltpu.VMEM((size, packed, LANES), BF16),
        pltpu.VMEM((size, positions // size, positions), BF16),
        pltpu.VMEM((size, positions // size, positions), BF16),
        dma, dma((CHUNKS,)), dma, dma((CHUNKS,)), dma, dma((CHUNKS,)), dma, dma((CHUNKS,)),
        dma((2,)), dma((2,)),
    ]
    results = pl.pallas_call(
        functools.partial(kernel, groups),
        out_shape=outs,
        in_specs=[vmem] * 7,
        out_specs=(vmem,) * 7,
        scratch_shapes=scratch,
        compiler_params=pltpu.CompilerParams(
            collective_id=0, has_side_effects=True, vmem_limit_bytes=67043328
        ),
    )(signal, factor_first[0], factor_second[0], up_weight[0], down_weight[0], norm_gain, cotangent)
    gain = results[6][:1, : width // size]
    return results[:2] + tuple(value[None] for value in results[2:6]) + (gain,)


def solution(mesh):
    placed = (
        P("ctx", None, "ch"),
        P("ch", None, None),
        P("ch", None, None),
        P("ch", None, None),
        P("ch", None, None),
        P("ch", None),
        P("ctx", None, "ch"),
    )
    return jax.shard_map(
        functools.partial(shards, mesh),
        mesh=mesh,
        in_specs=placed,
        out_specs=(
            P("ctx", None, "ch"),
            P("ctx", None, "ch"),
            P("ch", "ctx", None),
            P("ch", "ctx", None),
            P("ch", "ctx", None),
            P("ch", "ctx", None),
            P("ch", "ctx"),
        ),
        check_vma=False,
    )
```

time: 934 us -> 121 us (0.13)
  waiting for transfers between devices: 672 us -> 0 us
  Pallas kernels: 0 us -> 112 us
  blocking collectives: 110 us -> 0 us
  matrix products: 82.9 us -> 0 us
  local copies, waits for them, and re-layouts: 26.1 us -> 8.22 us
  between operations: 15.3 us -> 0.66 us
  other arithmetic: 13.8 us -> 0 us
  starting transfers between devices: 13.8 us -> 0 us
    reduce_scatter x3 -> x0, waiting for transfers between devices: 335 us -> none  [the longest x1 161 us: shards(): lax.psum_scatter(grad_up, 'ctx', scatter_dimension=1, tiled=True)]
    unnamed x5 -> x0, waiting for transfers between devices: 308 us -> none
    pallas_call x0 -> x1, Pallas kernels: none -> 112 us  [shards(): pl.pallas_call(functools.partial(kernel, groups), out_shape=outs, in_spec...]
    unnamed x1 -> x0, blocking collectives: 83.5 us -> none
    dot_general x12 -> x0, matrix products: 82.9 us -> none  [the longest x1 15 us: shards(): jnp.einsum('jigc,ghc->jigh', upstream, down_weight, preferred_element_typ...]
    all_to_all x2 -> x0, waiting for transfers between devices: 28.2 us -> none  [transpose_slab(): return lax.all_to_all(block, 'ctx', split_axis=1, concat_axis=0, tiled=True)]
    psum x2 -> x0, blocking collectives: 26.4 us -> none  [channel_total(): return lax.psum(partial_value, 'ch')]
    all_to_all x2 -> x0, starting transfers between devices: 13.4 us -> none  [transpose_slab(): return lax.all_to_all(block, 'ctx', split_axis=1, concat_axis=0, tiled=True)]
  transfers between devices with their start and end apart: 6 -> 0, of which waited for: 5 -> 0; matrix products, arithmetic and copies ran while one was open for 7% -> 0% of each run, Pallas kernels for 0% -> 0%
where the time goes in v1:
time: 121 us
  Pallas kernels  112 us (93%)
  local copies, waits for them, and re-layouts  8.22 us (7%)
    pallas_call x1, Pallas kernels, shards(): pl.pallas_call(functools.partial(kernel, groups), out_shape=outs, in_spec...  112 us
    unnamed x16, local copies, waits for them, and re-layouts  7.03 us

profile of v1, /device:TPU:0, one launch (start us, length us, event | category | flops | bytes accessed | tf_op | source)
XLA Modules:
  0.0 120.9 jit_solution(12332334941602387998)
XLA Ops:
  0.6 112.0 %shard_map.126 = (bf16[16,256,256]{2,1,0:T(8,128)(2,1)}, bf16[8,512,256]{2,1,0:T(8,128)(2,1)}, f32[16,512]{1,0:T(8,128)}, f32[8,256]{1,0:T(8,128)}, f32[8,1024]{...) custom-call(bf16[8,512,256]{2,1,0:T(8,128)(2,1)} %signal.1, bf16[512,512]{1,0:T(8,128)(2,1)} %bitcast.8, ...), custom_call_target="tpu_custom_call" | custom-call | tf_op jit(solution)/shard_map/pallas_call | solution.py:453
  112.7 1.2 slice.3
  113.9 0.0 copy-start
  113.9 3.2 %copy.20 = bf16[16,256,256]{2,1,0:T(8,128)(2,1)} copy(bf16[16,256,256]{2,1,0:T(8,128)(2,1)} %get-tuple-element.28) | data formatting | bytes 4194304
  117.1 0.0 copy-done
  117.1 0.0 copy-start.3
  117.1 0.0 copy-start.4
  117.1 0.0 copy-start.2
  117.1 0.0 copy-start.1
  117.1 1.3 %copy.21 = bf16[8,512,256]{2,1,0:T(8,128)(2,1)} copy(bf16[8,512,256]{2,1,0:T(8,128)(2,1)S(1)} %copy-done) | data formatting | bytes 4194304
  118.5 0.0 copy-done.3
  118.5 0.6 copy.22
  119.1 0.0 copy-done.4
  119.1 0.6 copy.23
  119.7 0.0 copy-done.2
  119.7 0.6 copy.24
  120.3 0.0 copy-done.1
  120.3 0.6 copy.25
Async XLA Ops:
  113.9 3.2 %copy-start = (bf16[8,512,256]{2,1,0:T(8,128)(2,1)S(1)}, bf16[8,512,256]{2,1,0:T(8,128)(2,1)}, u32[]{:S(2)}) copy-start(bf16[8,512,256]{2,1,0:T(8,128)(2,1)} %get-tuple-element.29) | copy-start | bytes 6291460
  117.1 1.3 %copy-start.3 = (f32[16,512]{1,0:T(8,128)S(1)}, f32[16,512]{1,0:T(8,128)}, u32[]{:S(2)}) copy-start(f32[16,512]{1,0:T(8,128)} %get-tuple-element.16) | copy-start | bytes 98308
  117.1 2.0 %copy-start.4 = (f32[8,256]{1,0:T(8,128)S(1)}, f32[8,256]{1,0:T(8,128)}, u32[]{:S(2)}) copy-start(f32[8,256]{1,0:T(8,128)} %get-tuple-element.17) | copy-start | bytes 24580
  117.1 2.6 %copy-start.2 = (f32[8,1024]{1,0:T(8,128)S(1)}, f32[8,1024]{1,0:T(8,128)}, u32[]{:S(2)}) copy-start(f32[8,1024]{1,0:T(8,128)} %get-tuple-element.18) | copy-start | bytes 98308
  117.1 3.2 %copy-start.1 = (f32[32,256]{1,0:T(8,128)S(1)}, f32[32,256]{1,0:T(8,128)}, u32[]{:S(2)}) copy-start(f32[32,256]{1,0:T(8,128)} %get-tuple-element.19) | copy-start | bytes 98308

commit v2 on v1

v2 whole, which is shorter than its diff:
```python
import functools
import math

import jax
import jax.numpy as jnp
from jax import lax
from jax.experimental import pallas as pl
from jax.experimental.pallas import tpu as pltpu
from jax.sharding import PartitionSpec as P

D = 1024
EPSILON = 1e-05
CHUNKS = 4
LANES = 128
ROWS = 8
HIDDEN = 256
PAIR = 2
MESH = pl.DeviceIdType.MESH
BF16 = jnp.bfloat16
F32 = jnp.float32
CUBIC = 0.044715
SLOPE = math.sqrt(2.0 / math.pi)


def dot(lhs, rhs):
    return jnp.dot(lhs, rhs, preferred_element_type=F32)


def dot_rows(lhs, rhs):
    return lax.dot_general(lhs, rhs, (((0,), (0,)), ((), ())), preferred_element_type=F32)


def dot_columns(lhs, rhs):
    return lax.dot_general(lhs, rhs, (((1,), (1,)), ((), ())), preferred_element_type=F32)


def lane_blocks(value):
    return [value[..., at : at + LANES] for at in range(0, value.shape[-1], LANES)]


OUT = pltpu.VMEM
LIMIT = 61865984

def kernel(
    groups, signal_in, first_in, second_in, up_in, down_in, gain_in, cotangent_in,
    layer_out, grad_signal, out_first, out_second, out_up, out_down, out_gain,
    signal, first, second, up, down, gain, cotangent,
    first_t, second_t, up_t, down_t, first_mix, stage, send_one, recv_one, moved, mixed_all,
    scaled_all, grad_acts, squares, crosses, inverse_rows, inverse_wide, cross_wide, send_two,
    recv_two, unpacked, acc_up, acc_down, acc_second, acc_first, acc_gain, pack_up, got_up,
    pack_rest, got_rest, pack_first, got_first, load_sem, one_send, one_recv, two_send, two_recv,
    square_send, square_recv, cross_send, cross_recv, grad_send, grad_recv,
):
    me = lax.axis_index("ctx")
    channel = lax.axis_index("ch")
    local_a, positions, width = signal.shape
    local_j, rows, _ = cotangent.shape
    hidden = up.shape[1]
    size = rows // local_a
    span = local_j // CHUNKS
    block = stage.shape[1] // local_a - ROWS
    per_block = block // local_j
    blocks = positions // block
    pitch = block + ROWS
    chunk_rows = span * local_a
    halves = width // LANES
    grad_scale = 1.0 / math.sqrt(rows * positions)

    loads = [
        pltpu.make_async_copy(source, target, load_sem.at[k])
        for k, (source, target) in enumerate(
            zip(
                (first_in, signal_in, second_in, up_in, down_in, gain_in, cotangent_in),
                (first, signal, second, up, down, gain, cotangent),
            )
        )
    ]
    for load in loads:
        load.start()

    barrier = pltpu.get_barrier_semaphore()

    def greet(k, carry):
        pl.semaphore_signal(
            barrier, inc=1, device_id={"ctx": lax.rem(me + k, size)}, device_id_type=MESH
        )
        return carry

    lax.fori_loop(1, size, greet, 0)
    for k in range(1, groups):
        pl.semaphore_signal(
            barrier, inc=1, device_id={"ch": lax.rem(channel + k, groups)}, device_id_type=MESH
        )

    loads[0].wait()
    first_t[...] = first[...].T
    loads[1].wait()

    def first_block(at, carry):
        part = pl.ds(pl.multiple_of(at * block, block), block)
        weights = first_t[part, :]
        for a in range(local_a):
            mix = dot(weights, signal[a])
            first_mix[a, part, :] = mix
            gated = mix * lax.logistic(signal[a, part, :].astype(F32))
            for h, piece in enumerate(lane_blocks(gated)):
                stage[h, a * pitch : a * pitch + block, :] = piece

        def turn(k, inner):
            for h in range(halves):
                taken = [
                    stage.at[h][pl.ds(k * local_j + j, local_a, stride=pitch), :]
                    for j in range(local_j)
                ]
                send_one[at * per_block + k, :, h * LANES : (h + 1) * LANES] = jnp.concatenate(
                    taken, axis=0
                ).astype(BF16)
            return inner

        lax.fori_loop(0, per_block, turn, 0)
        return carry

    lax.fori_loop(0, blocks, first_block, 0)
    pl.semaphore_wait(barrier, size - 1 + groups - 1)

    half = size // 4

    def send_part(source, target, part, send_sem, recv_sem, odd, start, stop):
        def launch(k, carry):
            peer = lax.rem(me + 2 * k + odd, size)
            pltpu.make_async_remote_copy(
                src_ref=source.at[peer, part],
                dst_ref=target.at[me, part],
                send_sem=send_sem,
                recv_sem=recv_sem,
                device_id={"ctx": peer},
                device_id_type=MESH,
            ).start()
            return carry

        lax.fori_loop(start, stop, launch, 0)

    def send_near(source, target, part, send_sem, recv_sem):
        send_part(source, target, part, send_sem, recv_sem, 0, 1, 2 * half)
        pltpu.make_async_copy(source.at[me, part], target.at[me, part], recv_sem).start()

    def send_far(*route, start=0, stop=2):
        send_part(*route, 1, start * half, stop * half)

    def first_route(q):
        part = pl.ds(pl.multiple_of(q * chunk_rows, chunk_rows), chunk_rows)
        return send_one, recv_one, part, one_send, one_recv.at[q]

    def second_route(q):
        part = pl.ds(q * (span // 2), span // 2)
        return send_two, recv_two, part, two_send, two_recv.at[q]

    def grad_route(pack, got, index):
        part = pl.ds(0, pack.shape[1])
        return pack, got, part, grad_send.at[index], grad_recv.at[index]

    send_far(*first_route(0))
    send_near(*first_route(0))
    send_far(*first_route(1), stop=1)
    send_near(*first_route(1))
    for load in loads[2:]:
        load.wait()
    second_t[...] = second[...].T
    up_t[...] = up[...].T
    down[...] = (down[...].astype(F32) * 0.5).astype(BF16)
    down_t[...] = down[...].T
    acc_up[...] = jnp.zeros_like(acc_up)
    acc_down[...] = jnp.zeros_like(acc_down)
    acc_second[...] = jnp.zeros_like(acc_second)
    acc_first[...] = jnp.zeros_like(acc_first)
    acc_gain[...] = jnp.zeros_like(acc_gain)

    def grad_act_rows(j, carry):
        grad_acts[j] = dot(cotangent[j], down_t[...]).astype(BF16)
        return carry

    lax.fori_loop(0, local_j * 3 // 4, grad_act_rows, 0)

    lane = lax.broadcasted_iota(jnp.int32, (rows, LANES), 1)

    def exchange(table, q, columns, send_sem, recv_sem):
        table[q, channel] = columns.T[:ROWS]
        for k in range(1, groups):
            pltpu.make_async_remote_copy(
                src_ref=table.at[q, channel],
                dst_ref=table.at[q, channel],
                send_sem=send_sem,
                recv_sem=recv_sem.at[q],
                device_id={"ch": lax.rem(channel + k, groups)},
                device_id_type=MESH,
            ).start()

    def collect(table, q, recv_sem):
        if groups > 1:
            others = table.at[q, : groups - 1]
            pltpu.make_async_copy(others, others, recv_sem.at[q]).wait()
        total = table[q, 0]
        for k in range(1, groups):
            total = total + table[q, k]
        return total / D

    def spread(values, wide, at):
        tall = jnp.concatenate([values] * (LANES // ROWS), axis=0).T
        for k in range(span):
            wide[at + k] = jnp.broadcast_to(tall[:, k : k + 1], (rows, LANES))

    def mix_chunk(q):
        part = pl.ds(pl.multiple_of(q * chunk_rows, chunk_rows), chunk_rows)
        arrived = recv_one.at[:, part]
        pltpu.make_async_copy(arrived, arrived, one_recv.at[q]).wait()
        columns = jnp.zeros((rows, LANES), F32)
        for pair in range(span // 2):
            at = pl.multiple_of(q * chunk_rows + pair * 2 * local_a, 2 * local_a)
            both = recv_one[:, pl.ds(at, 2 * local_a), :].astype(F32)
            for odd in range(2):
                k = 2 * pair + odd
                rows_k = both[:, odd * local_a : (odd + 1) * local_a, :]
                rows_k = rows_k.reshape(rows, width).astype(BF16)
                moved[q * span + k] = rows_k
                mixed = dot(second_t[...], rows_k)
                mixed_all[q * span + k] = mixed
                total = jnp.sum(mixed * mixed, axis=1, keepdims=True)
                columns = jnp.where(lane == k, total, columns)
        exchange(squares, q, columns, square_send, square_recv)

    def mlp_tile(q, step):
        j = q * span + step * PAIR
        slot = lax.rem(q, 2) * span + step * PAIR
        count = PAIR * rows
        mixed = mixed_all[pl.ds(j, PAIR)].reshape(count, width)
        wide = inverse_wide[pl.ds(slot, PAIR)].reshape(count, LANES)
        scaled = mixed * jnp.concatenate([wide] * halves, axis=1)
        gains = gain[...]
        normed = (scaled * gains).astype(BF16)
        upstream = cotangent[pl.ds(j, PAIR)].reshape(count, width)
        out = mixed
        grad_normed = None
        parts = [slice(at, at + HIDDEN) for at in range(0, hidden, HIDDEN)]
        ready = dot(normed, up[:, parts[0]])
        for n, part in enumerate(parts):
            pre = ready
            if n + 1 < len(parts):
                ready = dot(normed, up[:, parts[n + 1]])
            grad_act = grad_acts[pl.ds(j, PAIR), :, part].reshape(count, HIDDEN).astype(F32)
            base = SLOPE + (SLOPE * CUBIC) * (pre * pre)
            curve = jnp.tanh(pre * base)
            opened = 1.0 + curve
            act = (pre * opened).astype(BF16)
            bend = pre * (3.0 * base - 2.0 * SLOPE)
            grad_pre = (grad_act * (opened * (1.0 + (1.0 - curve) * bend))).astype(BF16)
            out = out + dot(act, down[part, :])
            back = dot(grad_pre, up_t[part, :])
            grad_normed = back if grad_normed is None else grad_normed + back
            acc_down[:, part] += dot_rows(upstream, act)
            acc_up[:, part] += dot_rows(normed, grad_pre)
        layer_out[pl.ds(j, PAIR)] = out.astype(BF16).reshape(PAIR, rows, width)
        acc_gain[...] += jnp.sum(
            (grad_normed * scaled).reshape(count // ROWS, ROWS, width), axis=0
        )
        grad_scaled = grad_normed * gains
        scaled_all[pl.ds(j, PAIR)] = grad_scaled.reshape(PAIR, rows, width)
        total = jnp.sum(grad_scaled * mixed, axis=1, keepdims=True)
        cross_wide[pl.ds(slot, PAIR)] = jnp.broadcast_to(total, (count, LANES)).reshape(
            PAIR, rows, LANES
        )

    def send_cross(q):
        at = lax.rem(q, 2) * span
        columns = jnp.zeros((rows, LANES), F32)
        for k in range(span):
            columns = jnp.where(lane == k, cross_wide[at + k], columns)
        exchange(crosses, q, columns, cross_send, cross_recv)

    def back_chunk(q):
        at = lax.rem(q, 2) * span
        inverse = inverse_rows[lax.rem(q, 2)]
        spread(collect(crosses, q, cross_recv) * inverse * inverse * inverse, cross_wide, at)
        for pair in range(span // 2):
            turned = []
            for odd in range(2):
                k = 2 * pair + odd
                j = q * span + k
                wide = jnp.concatenate([inverse_wide[at + k]] * halves, axis=1)
                pull = jnp.concatenate([cross_wide[at + k]] * halves, axis=1)
                grad_mixed = (
                    cotangent[j].astype(F32) + wide * scaled_all[j] - pull * mixed_all[j]
                ).astype(BF16)
                acc_second[...] += dot_columns(moved[j], grad_mixed)
                turned.append(dot(second[...], grad_mixed).reshape(size, local_a, width))
            send_two[:, q * (span // 2) + pair] = jnp.concatenate(turned, axis=1).astype(BF16)

    mix_chunk(0)
    send_far(*first_route(1), start=1)
    send_far(*first_route(2), stop=1)
    send_near(*first_route(2))
    lax.fori_loop(local_j * 3 // 4, local_j, grad_act_rows, 0)

    def chunk(q, carry):
        inverse = lax.rsqrt(collect(squares, q, square_recv) + EPSILON)
        inverse_rows[lax.rem(q, 2)] = inverse
        spread(inverse, inverse_wide, lax.rem(q, 2) * span)

        def tile(step, inner):
            mlp_tile(q, step)

            @pl.when((step == 0) & (q < CHUNKS - 1))
            def _():
                mix_chunk(q + 1)

            @pl.when((step == 0) & (q < CHUNKS - 2))
            def _():
                send_far(*first_route(q + 2), start=1)

            @pl.when((step == 0) & (q < CHUNKS - 3))
            def _():
                send_far(*first_route(q + 3), stop=1)
                send_near(*first_route(q + 3))

            @pl.when((step == 0) & (q > 0))
            def _():
                back_chunk(q - 1)
                send_near(*second_route(q - 1))

            return inner

        lax.fori_loop(0, span // PAIR, tile, 0)
        send_cross(q)

        @pl.when(q > 0)
        def _():
            send_far(*second_route(q - 1))

        return carry

    lax.fori_loop(0, CHUNKS, chunk, 0)

    def pack(target, pieces):
        at = 0
        while pieces:
            joined = pieces.pop(0)
            if joined.shape[1] % 16:
                joined = jnp.concatenate([joined, pieces.pop(0)], axis=1)
            target[:, at : at + joined.shape[1], :] = joined.astype(BF16)
            at += joined.shape[1]

    pack(pack_up, lane_blocks(acc_up[...].reshape(size, width // size, hidden)))
    send_near(*grad_route(pack_up, got_up, 0))
    back_chunk(CHUNKS - 1)
    send_far(*second_route(CHUNKS - 1))
    send_near(*second_route(CHUNKS - 1))
    send_far(*grad_route(pack_up, got_up, 0))

    seconds = lane_blocks(acc_second[...].reshape(size, local_a, rows))
    downs = lane_blocks((acc_down[...] * 0.5).T.reshape(size, hidden // size, width))
    gain_row = jnp.sum(acc_gain[...], axis=0, keepdims=True)
    gains = [
        jnp.broadcast_to(piece[None], (size, ROWS, LANES)) for piece in lane_blocks(gain_row)
    ]
    pack(pack_rest, seconds + downs + gains)
    send_far(*grad_route(pack_rest, got_rest, 1))
    send_near(*grad_route(pack_rest, got_rest, 1))

    chunk_height = span * local_a
    for q in range(CHUNKS):
        arrived = recv_two.at[:, q * (span // 2) : (q + 1) * (span // 2)]
        pltpu.make_async_copy(arrived, arrived, two_recv.at[q]).wait()

        def unpack(k, carry):
            value = recv_two[k, q * (span // 2) : (q + 1) * (span // 2)].astype(F32)
            value = value.reshape(chunk_height, width)
            at = pl.multiple_of(k * local_j * local_a + q * chunk_height, chunk_height)
            for h, piece in enumerate(lane_blocks(value)):
                unpacked[h, pl.ds(at, chunk_height), :] = piece
            return carry

        lax.fori_loop(0, size, unpack, 0, unroll=4)

    def back_row(step, carry):
        for odd in range(2):
            a = step * 2 + odd
            grad_gated = jnp.concatenate(
                [
                    unpacked.at[h][pl.ds(a, positions, stride=local_a), :]
                    for h in range(halves)
                ],
                axis=1,
            )
            inputs = signal[a]
            gate = lax.logistic(inputs.astype(F32))
            opened = grad_gated * gate
            grad_mix = opened.astype(BF16)
            grad_gate = opened * first_mix[a] * (1.0 - gate)
            grad_signal[a] = (dot(first[...], grad_mix) + grad_gate).astype(BF16)
            acc_first[...] += dot_columns(inputs, grad_mix)
        return carry

    lax.fori_loop(0, local_a // 2, back_row, 0)
    pack_first[...] = acc_first[...].reshape(pack_first.shape).astype(BF16)
    send_far(*grad_route(pack_first, got_first, 2))
    send_near(*grad_route(pack_first, got_first, 2))

    def gather(got, index):
        pltpu.make_async_copy(got, got, grad_recv.at[index]).wait()

        def add(k, total):
            return total + got[k].astype(F32)

        zero = jnp.zeros(got.shape[1:], F32)
        return lax.fori_loop(0, size, add, zero, unroll=4) * grad_scale

    def unfold(out, total, at):
        height = out.shape[0]
        for h in range(out.shape[1] // LANES):
            out[:, h * LANES : (h + 1) * LANES] = total[at : at + height]
            at += height
        return at

    unfold(out_up, gather(got_up, 0), 0)
    total = gather(got_rest, 1)
    at = unfold(out_second, total, 0)
    at = unfold(out_down, total, at)
    gain_sum = jnp.concatenate(
        [total[at + h * ROWS : at + (h + 1) * ROWS] for h in range(halves)], axis=1
    )
    turn = lax.rem(width - me * (width // size), width)
    out_gain[...] = pltpu.roll(gain_sum, turn, 1)[:, :LANES]
    out_first[...] = gather(got_first, 2)

    def drain(ref, sem):
        pltpu.make_async_copy(ref, ref, sem).wait()

    drain(send_one.at[: size - 1], one_send)
    drain(send_two.at[: size - 1], two_send)
    drain(pack_up.at[: size - 1], grad_send.at[0])
    drain(pack_rest.at[: size - 1], grad_send.at[1])
    drain(pack_first.at[: size - 1], grad_send.at[2])
    if groups > 1:
        drain(squares.at[:, : groups - 1], square_send)
        drain(crosses.at[:, : groups - 1], cross_send)


def finish(*refs):
    sources, targets, sems = refs[:7], refs[7:14], refs[14]
    copies = [
        pltpu.make_async_copy(sources[k], targets[k], sems.at[k]) for k in range(6)
    ]
    for copy in copies:
        copy.start()
    targets[6][...] = sources[6][:1, : targets[6].shape[1]]
    for copy in copies:
        copy.wait()


def shards(mesh, signal, factor_first, factor_second, up_weight, down_weight, norm_gain, cotangent):
    size, groups = mesh.shape["ctx"], mesh.shape["ch"]
    local_a, positions, width = signal.shape
    local_j, rows, _ = cotangent.shape
    hidden = up_weight.shape[2]
    halves = width // LANES
    span = local_j // CHUNKS
    block = min(128, positions)
    vmem = pl.BlockSpec(memory_space=pltpu.VMEM)
    anywhere = pl.BlockSpec(memory_space=pl.ANY)
    up_rows = width // size * (hidden // LANES)
    rest_rows = local_a * (rows // LANES) + hidden // size * halves + ROWS * halves

    results = (
        (cotangent.shape, BF16),
        (signal.shape, BF16),
        ((positions // size, positions), F32),
        ((rows // size, rows), F32),
        ((width // size, hidden), F32),
        ((hidden // size, width), F32),
    )
    dma = pltpu.SemaphoreType.DMA
    scratch = [
        pltpu.VMEM(signal.shape, BF16),
        pltpu.VMEM((positions, positions), BF16),
        pltpu.VMEM((rows, rows), BF16),
        pltpu.VMEM((width, hidden), BF16),
        pltpu.VMEM((hidden, width), BF16),
        pltpu.VMEM((1, width), F32),
        pltpu.VMEM(cotangent.shape, BF16),
        pltpu.VMEM((positions, positions), BF16),
        pltpu.VMEM((rows, rows), BF16),
        pltpu.VMEM((hidden, width), BF16),
        pltpu.VMEM((width, hidden), BF16),
        pltpu.VMEM((local_a, positions, width), F32),
        pltpu.VMEM((halves, local_a * (block + ROWS), LANES), F32),
        pltpu.VMEM((size, local_j * local_a, width), BF16),
        pltpu.VMEM((size, local_j * local_a, width), BF16),
        pltpu.VMEM((local_j, rows, width), BF16),
        pltpu.VMEM((local_j, rows, width), F32),
        pltpu.VMEM((local_j, rows, width), F32),
        pltpu.VMEM((local_j, rows, hidden), BF16),
        pltpu.VMEM((CHUNKS, groups, ROWS, rows), F32),
        pltpu.VMEM((CHUNKS, groups, ROWS, rows), F32),
        pltpu.VMEM((2, ROWS, rows), F32),
        pltpu.VMEM((2 * span, rows, LANES), F32),
        pltpu.VMEM((2 * span, rows, LANES), F32),
        pltpu.VMEM((size, local_j // 2, 2 * local_a, width), BF16),
        pltpu.VMEM((size, local_j // 2, 2 * local_a, width), BF16),
        pltpu.VMEM((halves, positions * local_a, LANES), F32),
        pltpu.VMEM((width, hidden), F32),
        pltpu.VMEM((width, hidden), F32),
        pltpu.VMEM((rows, rows), F32),
        pltpu.VMEM((positions, positions), F32),
        pltpu.VMEM((ROWS, width), F32),
        pltpu.VMEM((size, up_rows, LANES), BF16),
        pltpu.VMEM((size, up_rows, LANES), BF16),
        pltpu.VMEM((size, rest_rows, LANES), BF16),
        pltpu.VMEM((size, rest_rows, LANES), BF16),
        pltpu.VMEM((size, positions // size, positions), BF16),
        pltpu.VMEM((size, positions // size, positions), BF16),
        dma((7,)), dma, dma((CHUNKS,)), dma, dma((CHUNKS,)), dma, dma((CHUNKS,)), dma,
        dma((CHUNKS,)), dma((3,)), dma((3,)),
    ]
    values = pl.pallas_call(
        functools.partial(kernel, groups),
        out_shape=tuple(OUT(*result) for result in results) + (OUT((ROWS, LANES), F32),),
        in_specs=[anywhere] * 7,
        out_specs=(vmem,) * 7,
        scratch_shapes=scratch,
        compiler_params=pltpu.CompilerParams(
            collective_id=0, has_side_effects=True, vmem_limit_bytes=LIMIT
        ),
    )(signal, factor_first[0], factor_second[0], up_weight[0], down_weight[0], norm_gain, cotangent)
    shapes = [jax.ShapeDtypeStruct(*result) for result in results]
    values = pl.pallas_call(
        finish,
        out_shape=(*shapes, jax.ShapeDtypeStruct((1, width // size), F32)),
        in_specs=[vmem] * 7,
        out_specs=(anywhere,) * 6 + (vmem,),
        scratch_shapes=[dma((6,))],
        compiler_params=pltpu.CompilerParams(vmem_limit_bytes=4194304),
    )(*[pltpu.with_memory_space_constraint(value, pltpu.VMEM) for value in values])
    return (*values[:2], *(value[None] for value in values[2:6]), values[6])


def solution(mesh):
    placed = (
        P("ctx", None, "ch"),
        P("ch", None, None),
        P("ch", None, None),
        P("ch", None, None),
        P("ch", None, None),
        P("ch", None),
        P("ctx", None, "ch"),
    )
    return jax.shard_map(
        functools.partial(shards, mesh),
        mesh=mesh,
        in_specs=placed,
        out_specs=(
            P("ctx", None, "ch"),
            P("ctx", None, "ch"),
            P("ch", "ctx", None),
            P("ch", "ctx", None),
            P("ch", "ctx", None),
            P("ch", "ctx", None),
            P("ch", "ctx"),
        ),
        check_vma=False,
    )
```

time: 121 us -> 91.4 us (0.76)
  Pallas kernels: 112 us -> 90.1 us
  local copies, waits for them, and re-layouts: 8.22 us -> 0 us
    pallas_call x1 -> x2, Pallas kernels: 112 us -> 90.1 us  [the longest x1 87.5 us: shards(): pl.pallas_call(functools.partial(kernel, groups), out_shape=tuple((OUT(*r...]
    unnamed x16 -> x0, local copies, waits for them, and re-layouts: 7.03 us -> none
where the time goes in v2:
time: 91.4 us; the launch traced here: 90.7 us
  Pallas kernels  90.1 us (99%)
    pallas_call x1, Pallas kernels, shards(): pl.pallas_call(functools.partial(kernel, groups), out_shape=tuple((OUT(*r...  87.5 us
    pallas_call x1, Pallas kernels, shards(): pl.pallas_call(finish, out_shape=(*shapes, jax.ShapeDtypeStruct((1, width...  2.58 us

profile of v2, /device:TPU:0, one launch (start us, length us, event | category | flops | bytes accessed | tf_op | source)
XLA Modules:
  0.0 90.7 jit_solution(12932232052546663054)
XLA Ops:
  0.6 87.5 %shard_map.126 = (bf16[16,256,256]{2,1,0:T(8,128)(2,1)S(1)}, bf16[8,512,256]{2,1,0:T(8,128)(2,1)S(1)}, f32[16,512]{1,0:T(8,128)S(1)}, f32[8,256]{1,0:T(8,128)S(1...) custom-call(bf16[8,512,256]{2,1,0:T(8,128)(2,1)} %signal_in.1, bf16[512,512]{1,0:T(8,128)(2,1)} %bitcast.8, ...), custom_call_target="tpu_custom_call" | custom-call | tf_op jit(solution)/shard_map/pallas_call | solution.py:523
  88.1 2.6 %shard_map.127 = (bf16[16,256,256]{2,1,0:T(8,128)(2,1)}, bf16[8,512,256]{2,1,0:T(8,128)(2,1)}, f32[16,512]{1,0:T(8,128)}, f32[8,256]{1,0:T(8,128)}, f32[8,1024]{...) custom-call(bf16[16,256,256]{2,1,0:T(8,128)(2,1)S(1)} %get-tuple-element.21.refs_0_, ...), custom_call_target="tpu_custom_call" | custom-call | tf_op jit(solution)/shard_map/pallas_call | solution.py:534

commit v3 on v2

--- a/solution.py
+++ b/solution.py
@@ -15,6 +15,7 @@
 ROWS = 8
 HIDDEN = 256
 PAIR = 2
+STRIDE = 5
 MESH = pl.DeviceIdType.MESH
 BF16 = jnp.bfloat16
 F32 = jnp.float32
@@ -47,8 +48,8 @@
     signal, first, second, up, down, gain, cotangent,
     first_t, second_t, up_t, down_t, first_mix, stage, send_one, recv_one, moved, mixed_all,
     scaled_all, grad_acts, squares, crosses, inverse_rows, inverse_wide, cross_wide, send_two,
-    recv_two, unpacked, acc_up, acc_down, acc_second, acc_first, acc_gain, pack_up, got_up,
-    pack_rest, got_rest, pack_first, got_first, load_sem, one_send, one_recv, two_send, two_recv,
+    recv_two, unpacked, acc_up, acc_down, acc_second, acc_first, acc_gain, grad_mixes, pack_up,
+    got_far, pack_near, got_up, pack_rest, got_rest, pack_last, got_last, pack_first, got_first, load_sem, one_send, one_recv, two_send, two_recv,
     square_send, square_recv, cross_send, cross_recv, grad_send, grad_recv,
 ):
     me = lax.axis_index("ctx")
@@ -127,7 +128,7 @@
 
     def send_part(source, target, part, send_sem, recv_sem, odd, start, stop):
         def launch(k, carry):
-            peer = lax.rem(me + 2 * k + odd, size)
+            peer = lax.rem(me + 2 * lax.rem(STRIDE * k, size // 2) + odd, size)
             pltpu.make_async_remote_copy(
                 src_ref=source.at[peer, part],
                 dst_ref=target.at[me, part],
@@ -154,10 +155,6 @@
     def second_route(q):
         part = pl.ds(q * (span // 2), span // 2)
         return send_two, recv_two, part, two_send, two_recv.at[q]
-
-    def grad_route(pack, got, index):
-        part = pl.ds(0, pack.shape[1])
-        return pack, got, part, grad_send.at[index], grad_recv.at[index]
 
     send_far(*first_route(0))
     send_near(*first_route(0))
@@ -241,11 +238,11 @@
         out = mixed
         grad_normed = None
         parts = [slice(at, at + HIDDEN) for at in range(0, hidden, HIDDEN)]
-        ready = dot(normed, up[:, parts[0]])
+        queue = [dot(normed, up[:, parts[0]]), dot(normed, up[:, parts[1]])]
         for n, part in enumerate(parts):
-            pre = ready
-            if n + 1 < len(parts):
-                ready = dot(normed, up[:, parts[n + 1]])
+            pre = queue.pop(0)
+            if n + 2 < len(parts):
+                queue.append(dot(normed, up[:, parts[n + 2]]))
             grad_act = grad_acts[pl.ds(j, PAIR), :, part].reshape(count, HIDDEN).astype(F32)
             base = SLOPE + (SLOPE * CUBIC) * (pre * pre)
             curve = jnp.tanh(pre * base)
@@ -345,15 +342,58 @@
             joined = pieces.pop(0)
             if joined.shape[1] % 16:
                 joined = jnp.concatenate([joined, pieces.pop(0)], axis=1)
-            target[:, at : at + joined.shape[1], :] = joined.astype(BF16)
-            at += joined.shape[1]
+            height = joined.shape[1]
+            joined = joined.astype(BF16).reshape(size // 2, 2, height, LANES)
+            target[:, :, at : at + height, :] = joined
+            at += height
+
+    mine = lax.rem(me, 2)
+    other = 1 - mine
+    mate = me + 1 - 2 * mine
+    place = me // 2
+    places = size // 2
+
+    def send_mate(source, target, index):
+        pltpu.make_async_remote_copy(
+            src_ref=source,
+            dst_ref=target,
+            send_sem=grad_send.at[index],
+            recv_sem=grad_recv.at[index],
+            device_id={"ctx": mate},
+            device_id_type=MESH,
+        ).start()
+
+    def send_places(source, target, index):
+        def launch(k, carry):
+            there = lax.rem(place + STRIDE * k, places)
+            pltpu.make_async_remote_copy(
+                src_ref=source.at[there],
+                dst_ref=target.at[place],
+                send_sem=grad_send.at[index],
+                recv_sem=grad_recv.at[index],
+                device_id={"ctx": 2 * there + mine},
+                device_id_type=MESH,
+            ).start()
+            return carry
+
+        lax.fori_loop(1, places, launch, 0)
+        pltpu.make_async_copy(source.at[place], target.at[place], grad_recv.at[index]).start()
+
+    def arrive(got, index):
+        pltpu.make_async_copy(got, got, grad_recv.at[index]).wait()
+
+    def add_up(got):
+        def add(k, total):
+            return total + got[k].astype(F32)
+
+        return lax.fori_loop(0, got.shape[0], add, jnp.zeros(got.shape[1:], F32), unroll=4)
 
     pack(pack_up, lane_blocks(acc_up[...].reshape(size, width // size, hidden)))
-    send_near(*grad_route(pack_up, got_up, 0))
+
     back_chunk(CHUNKS - 1)
     send_far(*second_route(CHUNKS - 1))
     send_near(*second_route(CHUNKS - 1))
-    send_far(*grad_route(pack_up, got_up, 0))
+    send_mate(pack_up.at[:, other], got_far, 0)
 
     seconds = lane_blocks(acc_second[...].reshape(size, local_a, rows))
     downs = lane_blocks((acc_down[...] * 0.5).T.reshape(size, hidden // size, width))
@@ -362,8 +402,11 @@
         jnp.broadcast_to(piece[None], (size, ROWS, LANES)) for piece in lane_blocks(gain_row)
     ]
     pack(pack_rest, seconds + downs + gains)
-    send_far(*grad_route(pack_rest, got_rest, 1))
-    send_near(*grad_route(pack_rest, got_rest, 1))
+    send_places(pack_rest, got_rest, 2)
+
+    arrive(got_far, 0)
+    pack_near[...] = (pack_up[:, mine].astype(F32) + got_far[...].astype(F32)).astype(BF16)
+    send_places(pack_near, got_up, 1)
 
     chunk_height = span * local_a
     for q in range(CHUNKS):
@@ -394,24 +437,28 @@
             gate = lax.logistic(inputs.astype(F32))
             opened = grad_gated * gate
             grad_mix = opened.astype(BF16)
-            grad_gate = opened * first_mix[a] * (1.0 - gate)
-            grad_signal[a] = (dot(first[...], grad_mix) + grad_gate).astype(BF16)
+            grad_mixes[a] = grad_mix
+            first_mix[a] = opened * first_mix[a] * (1.0 - gate)
             acc_first[...] += dot_columns(inputs, grad_mix)
         return carry
 
     lax.fori_loop(0, local_a // 2, back_row, 0)
     pack_first[...] = acc_first[...].reshape(pack_first.shape).astype(BF16)
-    send_far(*grad_route(pack_first, got_first, 2))
-    send_near(*grad_route(pack_first, got_first, 2))
-
-    def gather(got, index):
-        pltpu.make_async_copy(got, got, grad_recv.at[index]).wait()
-
-        def add(k, total):
-            return total + got[k].astype(F32)
-
-        zero = jnp.zeros(got.shape[1:], F32)
-        return lax.fori_loop(0, size, add, zero, unroll=4) * grad_scale
+    whole = pl.ds(0, pack_first.shape[1])
+    route = (pack_first, got_first, whole, grad_send.at[4], grad_recv.at[4])
+    send_far(*route)
+    send_near(*route)
+
+    arrive(got_rest, 2)
+    rest = add_up(got_rest)
+    pack_last[...] = jnp.where(mine == 0, rest[1], rest[0]).astype(BF16)
+    send_mate(pack_last, got_last, 3)
+
+    def signal_row(a, carry):
+        grad_signal[a] = (dot(first[...], grad_mixes[a]) + first_mix[a]).astype(BF16)
+        return carry
+
+    lax.fori_loop(0, local_a, signal_row, 0)
 
     def unfold(out, total, at):
         height = out.shape[0]
@@ -420,8 +467,11 @@
             at += height
         return at
 
-    unfold(out_up, gather(got_up, 0), 0)
-    total = gather(got_rest, 1)
+    arrive(got_up, 1)
+    unfold(out_up, add_up(got_up) * grad_scale, 0)
+    arrive(got_last, 3)
+    total = jnp.where(mine == 0, rest[0], rest[1])
+    total = (total + got_last[...].astype(F32)) * grad_scale
     at = unfold(out_second, total, 0)
     at = unfold(out_down, total, at)
     gain_sum = jnp.concatenate(
@@ -429,16 +479,19 @@
     )
     turn = lax.rem(width - me * (width // size), width)
     out_gain[...] = pltpu.roll(gain_sum, turn, 1)[:, :LANES]
-    out_first[...] = gather(got_first, 2)
+    arrive(got_first, 4)
+    out_first[...] = add_up(got_first) * grad_scale
 
     def drain(ref, sem):
         pltpu.make_async_copy(ref, ref, sem).wait()
 
     drain(send_one.at[: size - 1], one_send)
     drain(send_two.at[: size - 1], two_send)
-    drain(pack_up.at[: size - 1], grad_send.at[0])
-    drain(pack_rest.at[: size - 1], grad_send.at[1])
-    drain(pack_first.at[: size - 1], grad_send.at[2])
+    drain(got_far, grad_send.at[0])
+    drain(pack_near.at[: places - 1], grad_send.at[1])
+    drain(pack_rest.at[: places - 1], grad_send.at[2])
+    drain(pack_last, grad_send.at[3])
+    drain(pack_first.at[: size - 1], grad_send.at[4])
     if groups > 1:
         drain(squares.at[:, : groups - 1], square_send)
         drain(crosses.at[:, : groups - 1], cross_send)
@@ -511,14 +564,19 @@
         pltpu.VMEM((rows, rows), F32),
         pltpu.VMEM((positions, positions), F32),
         pltpu.VMEM((ROWS, width), F32),
-        pltpu.VMEM((size, up_rows, LANES), BF16),
-        pltpu.VMEM((size, up_rows, LANES), BF16),
-        pltpu.VMEM((size, rest_rows, LANES), BF16),
-        pltpu.VMEM((size, rest_rows, LANES), BF16),
+        pltpu.VMEM(signal.shape, BF16),
+        pltpu.VMEM((size // 2, 2, up_rows, LANES), BF16),
+        pltpu.VMEM((size // 2, up_rows, LANES), BF16),
+        pltpu.VMEM((size // 2, up_rows, LANES), BF16),
+        pltpu.VMEM((size // 2, up_rows, LANES), BF16),
+        pltpu.VMEM((size // 2, 2, rest_rows, LANES), BF16),
+        pltpu.VMEM((size // 2, 2, rest_rows, LANES), BF16),
+        pltpu.VMEM((rest_rows, LANES), BF16),
+        pltpu.VMEM((rest_rows, LANES), BF16),
         pltpu.VMEM((size, positions // size, positions), BF16),
         pltpu.VMEM((size, positions // size, positions), BF16),
         dma((7,)), dma, dma((CHUNKS,)), dma, dma((CHUNKS,)), dma, dma((CHUNKS,)), dma,
-        dma((CHUNKS,)), dma((3,)), dma((3,)),
+        dma((CHUNKS,)), dma((5,)), dma((5,)),
     ]
     values = pl.pallas_call(
         functools.partial(kernel, groups),

time: 91.4 us -> 89.6 us (0.980)
  Pallas kernels: 90.1 us -> 88.5 us
    pallas_call x1, Pallas kernels: 87.5 us -> 85.9 us  [shards(): pl.pallas_call(functools.partial(kernel, groups), out_shape=tuple((OUT(*r...]
where the time goes in v3:
time: 89.6 us; the launch traced here: 89.2 us
  Pallas kernels  88.5 us (99%)
    pallas_call x1, Pallas kernels, shards(): pl.pallas_call(functools.partial(kernel, groups), out_shape=tuple((OUT(*r...  85.9 us
    pallas_call x1, Pallas kernels, shards(): pl.pallas_call(finish, out_shape=(*shapes, jax.ShapeDtypeStruct((1, width...  2.58 us

profile of v3, /device:TPU:0, one launch (start us, length us, event | category | flops | bytes accessed | tf_op | source)
XLA Modules:
  0.0 89.2 jit_solution(2572178364826102181)
XLA Ops:
  0.6 85.9 %shard_map.126 = (bf16[16,256,256]{2,1,0:T(8,128)(2,1)S(1)}, bf16[8,512,256]{2,1,0:T(8,128)(2,1)S(1)}, f32[16,512]{1,0:T(8,128)S(1)}, f32[8,256]{1,0:T(8,128)S(1...) custom-call(bf16[8,512,256]{2,1,0:T(8,128)(2,1)} %signal_in.1, bf16[512,512]{1,0:T(8,128)(2,1)} %bitcast.8, ...), custom_call_target="tpu_custom_call" | custom-call | tf_op jit(solution)/shard_map/pallas_call | solution.py:581
  86.6 2.6 %shard_map.127 = (bf16[16,256,256]{2,1,0:T(8,128)(2,1)}, bf16[8,512,256]{2,1,0:T(8,128)(2,1)}, f32[16,512]{1,0:T(8,128)}, f32[8,256]{1,0:T(8,128)}, f32[8,1024]{...) custom-call(bf16[16,256,256]{2,1,0:T(8,128)(2,1)S(1)} %get-tuple-element.21.refs_0_, ...), custom_call_target="tpu_custom_call" | custom-call | tf_op jit(solution)/shard_map/pallas_call | solution.py:592

commit v4 on v3

--- a/solution.py
+++ b/solution.py
@@ -76,14 +76,17 @@
             )
         )
     ]
-    for load in loads:
+    for load in loads[:2]:
         load.start()
 
     barrier = pltpu.get_barrier_semaphore()
 
     def greet(k, carry):
         pl.semaphore_signal(
-            barrier, inc=1, device_id={"ctx": lax.rem(me + k, size)}, device_id_type=MESH
+            barrier,
+            inc=1,
+            device_id={"ctx": lax.rem(me + 1 + lax.rem(k + size // 2 + 2, size - 1), size)},
+            device_id_type=MESH,
         )
         return carry
 
@@ -96,6 +99,8 @@
     loads[0].wait()
     first_t[...] = first[...].T
     loads[1].wait()
+    for load in loads[2:]:
+        load.start()
 
     def first_block(at, carry):
         part = pl.ds(pl.multiple_of(at * block, block), block)
@@ -318,11 +323,6 @@
                 send_far(*first_route(q + 3), stop=1)
                 send_near(*first_route(q + 3))
 
-            @pl.when((step == 0) & (q > 0))
-            def _():
-                back_chunk(q - 1)
-                send_near(*second_route(q - 1))
-
             return inner
 
         lax.fori_loop(0, span // PAIR, tile, 0)
@@ -330,7 +330,9 @@
 
         @pl.when(q > 0)
         def _():
+            back_chunk(q - 1)
             send_far(*second_route(q - 1))
+            send_near(*second_route(q - 1))
 
         return carry
 

time: 89.6 us -> 88.2 us (0.984)
  Pallas kernels: 88.5 us -> 87 us
    pallas_call x1, Pallas kernels: 85.9 us -> 84.4 us  [shards(): pl.pallas_call(functools.partial(kernel, groups), out_shape=tuple((OUT(*r...]
where the time goes in v4:
time: 88.2 us; the launch traced here: 87.6 us
  Pallas kernels  87 us (99%)
    pallas_call x1, Pallas kernels, shards(): pl.pallas_call(functools.partial(kernel, groups), out_shape=tuple((OUT(*r...  84.4 us
    pallas_call x1, Pallas kernels, shards(): pl.pallas_call(finish, out_shape=(*shapes, jax.ShapeDtypeStruct((1, width...  2.58 us

profile of v4, /device:TPU:0, one launch (start us, length us, event | category | flops | bytes accessed | tf_op | source)
XLA Modules:
  0.0 87.6 jit_solution(8528278518033925072)
XLA Ops:
  0.6 84.4 %shard_map.126 = (bf16[16,256,256]{2,1,0:T(8,128)(2,1)S(1)}, bf16[8,512,256]{2,1,0:T(8,128)(2,1)S(1)}, f32[16,512]{1,0:T(8,128)S(1)}, f32[8,256]{1,0:T(8,128)S(1...) custom-call(bf16[8,512,256]{2,1,0:T(8,128)(2,1)} %signal_in.1, bf16[512,512]{1,0:T(8,128)(2,1)} %bitcast.8, ...), custom_call_target="tpu_custom_call" | custom-call | tf_op jit(solution)/shard_map/pallas_call | solution.py:583
  85.1 2.6 %shard_map.127 = (bf16[16,256,256]{2,1,0:T(8,128)(2,1)}, bf16[8,512,256]{2,1,0:T(8,128)(2,1)}, f32[16,512]{1,0:T(8,128)}, f32[8,256]{1,0:T(8,128)}, f32[8,1024]{...) custom-call(bf16[16,256,256]{2,1,0:T(8,128)(2,1)S(1)} %get-tuple-element.21.refs_0_, ...), custom_call_target="tpu_custom_call" | custom-call | tf_op jit(solution)/shard_map/pallas_call | solution.py:594
